TPU v7x, 32 devices: a whole 2x2x4 slice. The times are simulated.
32 devices in a mesh: dp: 8 (over y, x, core), tensor: 4 (over z).
Axes of the slice: x: 2, y: 2, z: 4, core: 2. Of those that a mesh axis runs over, the one named last changes fastest.
Arguments:
- target: bfloat16 [8192, 768], P('dp'), may hold values from -6 to 6
- memory: bfloat16 [8192, 768], P('dp'), may hold values from -6 to 6
- target_segments: int32 [8, 1024], P('dp'), may hold values from 0 to 4, as said below
- memory_segments: int32 [8, 1024], P('dp'), may hold values from 0 to 4, as said below
- self_query: bfloat16 [768, 768], P(None, 'tensor'), may hold values from -0.21875 to 0.21875
- self_query_bias: float32 [768], P('tensor'), may hold values from -3 to 3
- self_key: bfloat16 [768, 768], P(None, 'tensor'), may hold values from -0.21875 to 0.21875
- self_value: bfloat16 [768, 768], P(None, 'tensor'), may hold values from -0.21875 to 0.21875
- self_value_bias: float32 [768], P('tensor'), may hold values from -3 to 3
- self_output: bfloat16 [768, 768], P('tensor'), may hold values from -1.25 to 1.25
- self_output_bias: float32 [768], replicated, may hold values from -2 to 2
- first_gain: float32 [768], replicated, may hold values from 0.25 to 1.75
- first_shift: float32 [768], replicated, may hold values from -2 to 2
- cross_query: bfloat16 [768, 768], P(None, 'tensor'), may hold values from -0.21875 to 0.21875
- cross_query_bias: float32 [768], P('tensor'), may hold values from -3 to 3
- cross_key: bfloat16 [768, 768], P(None, 'tensor'), may hold values from -0.21875 to 0.21875
- cross_value: bfloat16 [768, 768], P(None, 'tensor'), may hold values from -0.21875 to 0.21875
- cross_value_bias: float32 [768], P('tensor'), may hold values from -3 to 3
- cross_output: bfloat16 [768, 768], P('tensor'), may hold values from -1.75 to 1.75
- cross_output_bias: float32 [768], replicated, may hold values from -2 to 2
- second_gain: float32 [768], replicated, may hold values from 0.25 to 1.75
- second_shift: float32 [768], replicated, may hold values from -2 to 2
- expand_weight: bfloat16 [768, 3072], P(None, 'tensor'), may hold values from -0.21875 to 0.21875
- expand_bias: float32 [3072], P('tensor'), may hold values from -3 to 3
- contract_weight: bfloat16 [3072, 768], P('tensor'), may hold values from -0.21875 to 0.21875
- contract_bias: float32 [768], replicated, may hold values from -2 to 2
- third_gain: float32 [768], replicated, may hold values from 0.25 to 1.75
- third_shift: float32 [768], replicated, may hold values from -2 to 2
- output_grad: bfloat16 [8192, 768], P('dp'), may hold values from -6 to 6
Outputs:
- layer_output: bfloat16 [8192, 768], P('dp')
- target_grad: bfloat16 [8192, 768], P('dp', 'tensor')
- memory_grad: bfloat16 [8192, 768], P('dp', 'tensor')
- grad_self_query: float32 [768, 768], P('dp', 'tensor')
- grad_self_query_bias: float32 [768], P('tensor')
- grad_self_key: float32 [768, 768], P('dp', 'tensor')
- grad_self_value: float32 [768, 768], P('dp', 'tensor')
- grad_self_value_bias: float32 [768], P('tensor')
- grad_self_output: float32 [768, 768], P('tensor', 'dp')
- grad_self_output_bias: float32 [768], replicated
- grad_first_gain: float32 [768], replicated
- grad_first_shift: float32 [768], replicated
- grad_cross_query: float32 [768, 768], P('dp', 'tensor')
- grad_cross_query_bias: float32 [768], P('tensor')
- grad_cross_key: float32 [768, 768], P('dp', 'tensor')
- grad_cross_value: float32 [768, 768], P('dp', 'tensor')
- grad_cross_value_bias: float32 [768], P('tensor')
- grad_cross_output: float32 [768, 768], P('tensor', 'dp')
- grad_cross_output_bias: float32 [768], replicated
- grad_second_gain: float32 [768], replicated
- grad_second_shift: float32 [768], replicated
- grad_expand_weight: float32 [768, 3072], P('dp', 'tensor')
- grad_expand_bias: float32 [3072], P('tensor')
- grad_contract_weight: float32 [3072, 768], P('tensor', 'dp')
- grad_contract_bias: float32 [768], replicated
- grad_third_gain: float32 [768], replicated
- grad_third_shift: float32 [768], replicated
Inputs may be any that keep to these rules, and one draw needn't show every extreme that they name: `target_segments`: along each row the ids never fall. Ids 0 to 3 are documents, every one present in every row with one or more positions; id 4 marks the padding at the row's end, 1 to 128 positions, and appears in every row. `memory_segments`: same law as target_segments, drawn independently: document d of a memory row belongs to document d of the same target row, and padding of target rows reads padding of memory rows.
All inputs are finite; a program needn't handle non-finite values.
Results may differ from a plain program's by a relative error of at most 0.025.
The roundings to bfloat16 on the way count: a program that leaves them out, or rounds other values in their place, can miss the bound.
Values sent between devices are 32-bit elements; how exact they have to be, the bound alone decides.
A program may use at most 128 MiB of HBM per device.

v0:
```python
from functools import partial
import jax
import jax.numpy as jnp
from jax import lax
from jax.sharding import PartitionSpec as P

HEAD_DIM = 64
EPSILON = 1e-05
NEGATIVE = -1e30


def normalize(summed, norm_gain, norm_shift):
    center = jnp.mean(summed, axis=-1, keepdims=True)
    centered = summed - center
    spread = jnp.mean(centered * centered, axis=-1, keepdims=True)
    return centered * lax.rsqrt(spread + EPSILON) * norm_gain + norm_shift


def exact_gelu(values):
    return jax.nn.gelu(values, approximate=False)


def matmul(left_side, right_side):
    return jnp.dot(left_side, right_side, preferred_element_type=jnp.float32)


def contract_rows(left_side, right_side):
    return lax.dot_general(
        left_side, right_side, (((0,), (0,)), ((), ())), preferred_element_type=jnp.float32
    )


def times_transpose(left_side, right_side):
    return lax.dot_general(
        left_side, right_side, (((1,), (1,)), ((), ())), preferred_element_type=jnp.float32
    )


def column_sums(values):
    return jnp.sum(values.astype(jnp.float32), axis=0)


def block_scores(chosen, key_rows, chosen_ids, key_ids, first_row, causal):
    block_rows = chosen.shape[0]
    allowed = chosen_ids[:, None] == key_ids[None, :]
    if causal:
        query_pos = first_row + jnp.arange(block_rows, dtype=jnp.int32)
        key_pos = jnp.arange(key_rows.shape[0], dtype=jnp.int32)
        allowed = allowed & (query_pos[:, None] >= key_pos[None, :])
    scores = jnp.einsum(
        "qhd,khd->hqk", chosen, key_rows, preferred_element_type=jnp.float32
    ) * chosen.shape[2] ** (-0.5)
    return jnp.where(allowed[None], scores, NEGATIVE)


def attend_row(causal, items):
    query_rows, key_rows, value_rows, query_ids, key_ids = items
    length = query_rows.shape[0]
    block_rows = min(512, length)

    def one_block(block_index):
        first_row = block_index * block_rows
        chosen = lax.dynamic_slice_in_dim(query_rows, first_row, block_rows, 0)
        chosen_ids = lax.dynamic_slice_in_dim(query_ids, first_row, block_rows, 0)
        scores = block_scores(chosen, key_rows, chosen_ids, key_ids, first_row, causal)
        row_max = jnp.max(scores, axis=-1, keepdims=True)
        exponent = jnp.exp(scores - row_max)
        row_sum = jnp.sum(exponent, axis=-1, keepdims=True)
        weights_low = (exponent / row_sum).astype(jnp.bfloat16)
        mixture = jnp.einsum(
            "hqk,khd->qhd", weights_low, value_rows, preferred_element_type=jnp.float32
        )
        return (mixture.astype(jnp.bfloat16), (row_max + jnp.log(row_sum))[..., 0])

    mixture, log_sums = lax.map(one_block, jnp.arange(length // block_rows, dtype=jnp.int32))
    return (mixture.reshape(query_rows.shape), log_sums)


def attend_back(causal, items):
    query_rows, key_rows, value_rows, query_ids, key_ids, log_sums, grad_mixture = items
    length = query_rows.shape[0]
    block_rows = min(512, length)
    score_scale = query_rows.shape[2] ** (-0.5)

    def one_block(carry, block_items):
        block_index, block_sums = block_items
        key_accum, value_accum = carry
        first_row = block_index * block_rows
        chosen = lax.dynamic_slice_in_dim(query_rows, first_row, block_rows, 0)
        chosen_ids = lax.dynamic_slice_in_dim(query_ids, first_row, block_rows, 0)
        chosen_grad = lax.dynamic_slice_in_dim(grad_mixture, first_row, block_rows, 0)
        scores = block_scores(chosen, key_rows, chosen_ids, key_ids, first_row, causal)
        weights_soft = jnp.exp(scores - block_sums[..., None])
        weights_low = weights_soft.astype(jnp.bfloat16)
        grad_weights = jnp.einsum(
            "qhd,khd->hqk", chosen_grad, value_rows, preferred_element_type=jnp.float32
        )
        row_dot = jnp.sum(weights_soft * grad_weights, axis=-1, keepdims=True)
        grad_scores = (weights_soft * (grad_weights - row_dot)).astype(jnp.bfloat16)
        grad_chosen = (
            jnp.einsum("hqk,khd->qhd", grad_scores, key_rows, preferred_element_type=jnp.float32)
            * score_scale
        )
        key_accum = (
            key_accum
            + jnp.einsum("hqk,qhd->khd", grad_scores, chosen, preferred_element_type=jnp.float32)
            * score_scale
        )
        value_accum = value_accum + jnp.einsum(
            "hqk,qhd->khd", weights_low, chosen_grad, preferred_element_type=jnp.float32
        )
        return ((key_accum, value_accum), grad_chosen.astype(jnp.bfloat16))

    zeros_start = jnp.zeros(key_rows.shape, jnp.float32)
    carried, grad_blocks = lax.scan(
        one_block,
        (zeros_start, zeros_start),
        (jnp.arange(length // block_rows, dtype=jnp.int32), log_sums),
    )
    return (
        grad_blocks.reshape(query_rows.shape),
        carried[0].astype(jnp.bfloat16),
        carried[1].astype(jnp.bfloat16),
    )


def per_device(
    target,
    memory,
    target_segments,
    memory_segments,
    self_query,
    self_query_bias,
    self_key,
    self_value,
    self_value_bias,
    self_output,
    self_output_bias,
    first_gain,
    first_shift,
    cross_query,
    cross_query_bias,
    cross_key,
    cross_value,
    cross_value_bias,
    cross_output,
    cross_output_bias,
    second_gain,
    second_shift,
    expand_weight,
    expand_bias,
    contract_weight,
    contract_bias,
    third_gain,
    third_shift,
    output_grad,
):
    row_count = target_segments.shape[0]
    local_width = self_query.shape[1]
    head_count = local_width // HEAD_DIM

    def to_heads(matrix):
        return matrix.reshape(row_count, -1, head_count, HEAD_DIM)

    def to_tokens(stacked):
        return stacked.reshape(-1, local_width)

    def branch_total(partial_term):
        return lax.psum(partial_term, "tensor")

    def input_total(partial_term):
        return lax.psum(partial_term, "tensor")

    def edge_total(partial_term):
        return lax.psum_scatter(partial_term, "tensor", scatter_dimension=1, tiled=True)

    self_queries = (matmul(target, self_query) + self_query_bias).astype(jnp.bfloat16)
    self_keys = matmul(target, self_key).astype(jnp.bfloat16)
    self_values = (matmul(target, self_value) + self_value_bias).astype(jnp.bfloat16)
    self_mixture, self_sums = lax.map(
        partial(attend_row, True),
        (
            to_heads(self_queries),
            to_heads(self_keys),
            to_heads(self_values),
            target_segments,
            target_segments,
        ),
    )
    self_mixed = to_tokens(self_mixture)
    self_branch = branch_total(matmul(self_mixed, self_output)) + self_output_bias
    first_norm, first_back = jax.vjp(
        normalize, target.astype(jnp.float32) + self_branch, first_gain, first_shift
    )
    first_low = first_norm.astype(jnp.bfloat16)
    cross_queries = (matmul(first_low, cross_query) + cross_query_bias).astype(jnp.bfloat16)
    cross_keys = matmul(memory, cross_key).astype(jnp.bfloat16)
    cross_values = (matmul(memory, cross_value) + cross_value_bias).astype(jnp.bfloat16)
    cross_mixture, cross_sums = lax.map(
        partial(attend_row, False),
        (
            to_heads(cross_queries),
            to_heads(cross_keys),
            to_heads(cross_values),
            target_segments,
            memory_segments,
        ),
    )
    cross_mixed = to_tokens(cross_mixture)
    cross_branch = branch_total(matmul(cross_mixed, cross_output)) + cross_output_bias
    second_norm, second_back = jax.vjp(
        normalize, first_norm + cross_branch, second_gain, second_shift
    )
    second_low = second_norm.astype(jnp.bfloat16)
    hidden = matmul(second_low, expand_weight) + expand_bias
    activated_float, gelu_back = jax.vjp(exact_gelu, hidden)
    activated = activated_float.astype(jnp.bfloat16)
    ffn_branch = branch_total(matmul(activated, contract_weight)) + contract_bias
    final_norm, third_back = jax.vjp(normalize, second_norm + ffn_branch, third_gain, third_shift)
    layer_output = final_norm.astype(jnp.bfloat16)
    grad_third_sum, grad_third_gain, grad_third_shift = third_back(output_grad.astype(jnp.float32))
    grad_ffn = grad_third_sum.astype(jnp.bfloat16)
    grad_contract_weight = contract_rows(activated, grad_ffn)
    grad_contract_bias = column_sums(grad_ffn)
    grad_hidden = gelu_back(times_transpose(grad_ffn, contract_weight))[0].astype(jnp.bfloat16)
    grad_expand_weight = contract_rows(second_low, grad_hidden)
    grad_expand_bias = column_sums(grad_hidden)
    ffn_summed = (grad_expand_weight, grad_contract_weight)
    grad_second = grad_third_sum + input_total(times_transpose(grad_hidden, expand_weight))
    grad_second_sum, grad_second_gain, grad_second_shift = second_back(grad_second)
    grad_cross = grad_second_sum.astype(jnp.bfloat16)
    grad_cross_output = contract_rows(cross_mixed, grad_cross)
    grad_cross_output_bias = column_sums(grad_cross)
    grad_cross_mixed = times_transpose(grad_cross, cross_output).astype(jnp.bfloat16)
    cross_grads = lax.map(
        partial(attend_back, False),
        (
            to_heads(cross_queries),
            to_heads(cross_keys),
            to_heads(cross_values),
            target_segments,
            memory_segments,
            cross_sums,
            to_heads(grad_cross_mixed),
        ),
    )
    grad_cross_queries = to_tokens(cross_grads[0])
    grad_cross_keys = to_tokens(cross_grads[1])
    grad_cross_values = to_tokens(cross_grads[2])
    grad_cross_query = contract_rows(first_low, grad_cross_queries)
    grad_cross_query_bias = column_sums(grad_cross_queries)
    grad_cross_key = contract_rows(memory, grad_cross_keys)
    grad_cross_value = contract_rows(memory, grad_cross_values)
    grad_cross_value_bias = column_sums(grad_cross_values)
    cross_summed = (grad_cross_query, grad_cross_key, grad_cross_value, grad_cross_output)
    memory_share = edge_total(
        times_transpose(grad_cross_keys, cross_key)
        + times_transpose(grad_cross_values, cross_value)
    )
    memory_grad = memory_share.astype(jnp.bfloat16)
    grad_first = grad_second_sum + input_total(times_transpose(grad_cross_queries, cross_query))
    grad_first_sum, grad_first_gain, grad_first_shift = first_back(grad_first)
    grad_self = grad_first_sum.astype(jnp.bfloat16)
    grad_self_output = contract_rows(self_mixed, grad_self)
    grad_self_output_bias = column_sums(grad_self)
    grad_self_mixed = times_transpose(grad_self, self_output).astype(jnp.bfloat16)
    self_grads = lax.map(
        partial(attend_back, True),
        (
            to_heads(self_queries),
            to_heads(self_keys),
            to_heads(self_values),
            target_segments,
            target_segments,
            self_sums,
            to_heads(grad_self_mixed),
        ),
    )
    grad_self_queries = to_tokens(self_grads[0])
    grad_self_keys = to_tokens(self_grads[1])
    grad_self_values = to_tokens(self_grads[2])
    grad_self_query = contract_rows(target, grad_self_queries)
    grad_self_query_bias = column_sums(grad_self_queries)
    grad_self_key = contract_rows(target, grad_self_keys)
    grad_self_value = contract_rows(target, grad_self_values)
    grad_self_value_bias = column_sums(grad_self_values)
    self_summed = (grad_self_query, grad_self_key, grad_self_value, grad_self_output)
    target_term = (
        times_transpose(grad_self_queries, self_query)
        + times_transpose(grad_self_keys, self_key)
        + times_transpose(grad_self_values, self_value)
    )
    target_share = edge_total(target_term)
    share_width = target_share.shape[1]
    residual_part = lax.dynamic_slice_in_dim(
        grad_first_sum, lax.axis_index("tensor") * share_width, share_width, 1
    )
    target_grad = (target_share + residual_part).astype(jnp.bfloat16)
    summed = (
        lax.psum_scatter(self_summed[0], "dp", scatter_dimension=0, tiled=True),
        lax.psum_scatter(self_summed[1], "dp", scatter_dimension=0, tiled=True),
        lax.psum_scatter(self_summed[2], "dp", scatter_dimension=0, tiled=True),
        lax.psum_scatter(self_summed[3], "dp", scatter_dimension=1, tiled=True),
        lax.psum_scatter(cross_summed[0], "dp", scatter_dimension=0, tiled=True),
        lax.psum_scatter(cross_summed[1], "dp", scatter_dimension=0, tiled=True),
        lax.psum_scatter(cross_summed[2], "dp", scatter_dimension=0, tiled=True),
        lax.psum_scatter(cross_summed[3], "dp", scatter_dimension=1, tiled=True),
        lax.psum_scatter(ffn_summed[0], "dp", scatter_dimension=0, tiled=True),
        lax.psum_scatter(ffn_summed[1], "dp", scatter_dimension=1, tiled=True),
    )
    vectors = lax.psum(
        (
            grad_self_query_bias,
            grad_self_value_bias,
            grad_self_output_bias,
            grad_first_gain,
            grad_first_shift,
            grad_cross_query_bias,
            grad_cross_value_bias,
            grad_cross_output_bias,
            grad_second_gain,
            grad_second_shift,
            grad_expand_bias,
            grad_contract_bias,
            grad_third_gain,
            grad_third_shift,
        ),
        "dp",
    )
    return (
        layer_output,
        target_grad,
        memory_grad,
        summed[0],
        vectors[0],
        summed[1],
        summed[2],
        vectors[1],
        summed[3],
        vectors[2],
        vectors[3],
        vectors[4],
        summed[4],
        vectors[5],
        summed[5],
        summed[6],
        vectors[6],
        summed[7],
        vectors[7],
        vectors[8],
        vectors[9],
        summed[8],
        vectors[10],
        summed[9],
        vectors[11],
        vectors[12],
        vectors[13],
    )


def solution(mesh):
    in_specs = (
        P("dp", None),
        P("dp", None),
        P("dp", None),
        P("dp", None),
        P(None, "tensor"),
        P("tensor"),
        P(None, "tensor"),
        P(None, "tensor"),
        P("tensor"),
        P("tensor", None),
        P(),
        P(),
        P(),
        P(None, "tensor"),
        P("tensor"),
        P(None, "tensor"),
        P(None, "tensor"),
        P("tensor"),
        P("tensor", None),
        P(),
        P(),
        P(),
        P(None, "tensor"),
        P("tensor"),
        P("tensor", None),
        P(),
        P(),
        P(),
        P("dp", None),
    )
    out_specs = (
        P("dp", None),
        P("dp", "tensor"),
        P("dp", "tensor"),
        P("dp", "tensor"),
        P("tensor"),
        P("dp", "tensor"),
        P("dp", "tensor"),
        P("tensor"),
        P("tensor", "dp"),
        P(),
        P(),
        P(),
        P("dp", "tensor"),
        P("tensor"),
        P("dp", "tensor"),
        P("dp", "tensor"),
        P("tensor"),
        P("tensor", "dp"),
        P(),
        P(),
        P(),
        P("dp", "tensor"),
        P("tensor"),
        P("tensor", "dp"),
        P(),
        P(),
        P(),
    )
    return jax.shard_map(
        per_device, mesh=mesh, in_specs=in_specs, out_specs=out_specs, check_vma=False
    )
```

profile of v0, /device:TPU:0, one launch (start us, length us, event | category | flops | bytes accessed | tf_op | source)
XLA Modules:
  0.0 1282.4 jit_solution(13164069724947715396)
XLA Ops:
  15.3 19.3 %while.96 = (s32[]{:T(128)}, bf16[2,512,3,64]{1,3,2,0:T(8,128)(2,1)}, f32[2,3,512]{2,1,0:T(4,128)}, s32[2]{0:T(128)S(1)}, s32[1024]{0:T(1024)S(1)}, /*index=5*/b...) while((s32[]{:T(128)}, ...), condition=%wide.region_3.4_spmd, body=%wide.region_0.3_spmd.sunk | while | flops 423197696 | bytes 27042136 | solution.py:75
  44.6 119.6 %all-reduce.7.cloned.1.call-done = f32[1024,768]{1,0:T(8,128)} async-done(((f32[1024,768]{1,0:T(8,128)}), f32[1024,768]{1,0:T(8,128)}) %all-reduce.7.cloned.1.call-update) | async-done | bytes 3145744 | tf_op jit(solution)/shard_map/psum | solution.py:169
  170.4 14.2 %while.97 = (s32[]{:T(128)}, bf16[2,512,3,64]{1,3,2,0:T(8,128)(2,1)S(1)}, f32[2,3,512]{2,1,0:T(4,128)S(1)}, s32[2]{0:T(128)S(1)}, s32[1024]{0:T(1024)S(1)}, /*in...) while((s32[]{:T(128)}, ...), condition=%wide.region_10.11_spmd, body=%wide.region_7.10_spmd.sunk | while | flops 422148608 | bytes 22221008 | solution.py:75
  190.3 119.8 %all-reduce.9.cloned.1.call-done = f32[1024,768]{1,0:T(8,128)} async-done(((f32[1024,768]{1,0:T(8,128)}), f32[1024,768]{1,0:T(8,128)}) %all-reduce.9.cloned.1.call-update) | async-done | bytes 3145744 | tf_op jit(solution)/shard_map/psum | solution.py:169
  316.2 9.8 multiply_convert_fusion.2
  330.3 120.2 %all-reduce.11.cloned.1.call-done = f32[1024,768]{1,0:T(8,128)} async-done(((f32[1024,768]{1,0:T(8,128)}), f32[1024,768]{1,0:T(8,128)}) %all-reduce.11.cloned.1.call-update) | async-done | bytes 3145744 | tf_op jit(solution)/shard_map/psum | solution.py:169
  471.0 120.0 %all-reduce.13.cloned.1.call-done = f32[1024,768]{1,0:T(8,128)} async-done(((f32[1024,768]{1,0:T(8,128)}), f32[1024,768]{1,0:T(8,128)}) %all-reduce.13.cloned.1.call-update) | async-done | bytes 3145744 | tf_op jit(solution)/shard_map/psum | solution.py:172
  591.0 5.4 multiply_reduce_fusion.2
  601.3 23.7 %while.98 = (s32[]{:T(128)}, f32[1024,3,64]{0,2,1:T(8,128)S(1)}, f32[1024,3,64]{0,2,1:T(8,128)}, bf16[2,512,3,64]{1,3,2,0:T(8,128)(2,1)}, s32[2]{0:T(128)S(1)}, ...) while((s32[]{:T(128)}, f32[1024,3,64]{0,2,1:T(8,128)S(1)}, ...), condition=%wide.region_24.25_spmd.clone, body=%wide.region_22.24_spmd.clone.sunk | while | flops 1031928320 | bytes 65659268 | solution.py:115
  634.3 115.9 %all-reduce.15.cloned.1.call-done = f32[1024,768]{1,0:T(8,128)} async-done(((f32[1024,768]{1,0:T(8,128)}), f32[1024,768]{1,0:T(8,128)}) %all-reduce.15.cloned.1.call-update) | async-done | bytes 3145744 | tf_op jit(solution)/shard_map/psum | solution.py:172
  750.2 5.4 multiply_reduce_fusion.3
  771.5 24.3 %while.99 = (s32[]{:T(128)}, f32[1024,3,64]{0,2,1:T(8,128)S(1)}, f32[1024,3,64]{0,2,1:T(8,128)}, bf16[2,512,3,64]{1,3,2,0:T(8,128)(2,1)}, s32[2]{0:T(128)S(1)}, ...) while((s32[]{:T(128)}, f32[1024,3,64]{0,2,1:T(8,128)S(1)}, ...), condition=%wide.region_30.31_spmd.clone, body=%wide.region_28.30_spmd.clone.sunk | while | flops 1032977408 | bytes 65663364 | solution.py:115
  807.7 5.6 fusion.106
  842.3 25.8 %all-reduce = (f32[192]{0:T(256)}, f32[192]{0:T(256)}, f32[768]{0:T(1024)}, f32[768]{0:T(1024)}, f32[768]{0:T(1024)}, /*index=5*/f32[192]{0:T(256)}, f32[192]{0:...) all-reduce(f32[192]{0:T(256)S(1)} %reduce_sum.341, ...), channel_id=1, replica_groups=mesh['dp'=8,'tensor'=4] {'dp'}, use_global_device_ids=true, to_apply=%region_35.36 | all-reduce | flops 8448 | bytes 67584 | tf_op jit(solution)/shard_map/psum | solution.py:311
  869.7 18.2 %reduce-scatter.29.cloned.1.call-done = f32[1024,192]{0,1:T(8,128)} async-done(((f32[1024,768]{0,1:T(8,128)}), f32[1024,192]{0,1:T(8,128)}) %reduce-scatter.29.cloned.1.call-update) | async-done | bytes 786448 | tf_op jit(solution)/shard_map/reduce_scatter | solution.py:175
  889.9 60.7 %reduce-scatter.37.cloned.1.call-done = f32[192,1024]{1,0:T(8,128)} async-done(((f32[768,1024]{1,0:T(8,128)}), f32[192,1024]{1,0:T(8,128)}) %reduce-scatter.37.cloned.1.call-update) | async-done | bytes 786448
  954.8 42.2 %reduce-scatter.35.cloned.1.call-done = f32[768,96]{0,1:T(8,128)} async-done(((f32[768,768]{0,1:T(8,128)}), f32[768,96]{0,1:T(8,128)}) %reduce-scatter.35.cloned.1.call-update) | async-done | bytes 294928 | tf_op jit(solution)/shard_map/reduce_scatter | solution.py:309
  996.9 46.8 %reduce-scatter.33.cloned.1.call-done = f32[96,768]{1,0:T(8,128)} async-done(((f32[768,768]{1,0:T(8,128)}), f32[96,768]{1,0:T(8,128)}) %reduce-scatter.33.cloned.1.call-update) | async-done | bytes 294928 | tf_op jit(solution)/shard_map/reduce_scatter | solution.py:308
  1043.7 38.6 %reduce-scatter.31.cloned.1.call-done = f32[96,192]{1,0:T(8,128)} async-done(((f32[768,192]{1,0:T(8,128)}), f32[96,192]{1,0:T(8,128)}) %reduce-scatter.31.cloned.1.call-update) | async-done | bytes 73744 | tf_op jit(solution)/shard_map/reduce_scatter | solution.py:304
  1082.3 38.7 %reduce-scatter.49.cloned.1.call-done = f32[96,192]{1,0:T(8,128)} async-done(((f32[768,192]{1,0:T(8,128)}), f32[96,192]{1,0:T(8,128)}) %reduce-scatter.49.cloned.1.call-update) | async-done | bytes 73744
  1121.1 38.6 %reduce-scatter.47.cloned.1.call-done = f32[96,192]{1,0:T(8,128)} async-done(((f32[768,192]{1,0:T(8,128)}), f32[96,192]{1,0:T(8,128)}) %reduce-scatter.47.cloned.1.call-update) | async-done | bytes 73744
  1159.7 38.6 %reduce-scatter.43.cloned.1.call-done = f32[96,192]{1,0:T(8,128)} async-done(((f32[768,192]{1,0:T(8,128)}), f32[96,192]{1,0:T(8,128)}) %reduce-scatter.43.cloned.1.call-update) | async-done | bytes 73744
  1198.3 38.6 %reduce-scatter.39.cloned.1.call-done = f32[96,192]{1,0:T(8,128)} async-done(((f32[768,192]{1,0:T(8,128)}), f32[96,192]{1,0:T(8,128)}) %reduce-scatter.39.cloned.1.call-update) | async-done | bytes 73744
  1236.9 38.6 %reduce-scatter.41.cloned.1.call-done = f32[96,192]{1,0:T(8,128)} async-done(((f32[768,192]{1,0:T(8,128)}), f32[96,192]{1,0:T(8,128)}) %reduce-scatter.41.cloned.1.call-update) | async-done | bytes 73744
  (451 shorter events, 213.9 us)
Async XLA Ops:
  7.2 157.0 %all-reduce.7.cloned.1.call-start = ((), (), s32[]{:S(2)}) async-start(), calls=%async_computation.12 | async-start | bytes 6291456 | tf_op jit(solution)/shard_map/psum | solution.py:169
  40.3 123.9 %copy-start.89 = (f32[768]{0:T(1024)S(1)}, f32[768]{0:T(1024)}, u32[]{:S(2)}) copy-start(f32[768]{0:T(1024)} %param.47) | copy-start | bytes 9220
  40.3 269.7 %all-reduce.9.cloned.1.call-start = ((), (), s32[]{:S(2)}) async-start(), calls=%async_computation.13 | async-start | bytes 6291456 | tf_op jit(solution)/shard_map/psum | solution.py:169
  168.2 141.9 %copy-start.58 = (f32[1024]{0:T(1024)}, f32[1024]{0:T(1024)S(1)}, u32[]{:S(2)}) copy-start(f32[1024]{0:T(1024)S(1)} %fusion.94) | copy-start | bytes 12292
  186.4 123.6 %copy-start.61 = (f32[768]{0:T(1024)S(1)}, f32[768]{0:T(1024)}, u32[]{:S(2)}) copy-start(f32[768]{0:T(1024)} %param.48) | copy-start | bytes 9220
  186.4 123.6 %copy-start.81 = (f32[768]{0:T(1024)S(1)}, f32[768]{0:T(1024)}, u32[]{:S(2)}) copy-start(f32[768]{0:T(1024)} %param.49) | copy-start | bytes 9220
  186.4 123.6 %copy-start.90 = (f32[768]{0:T(1024)S(1)}, f32[768]{0:T(1024)}, u32[]{:S(2)}) copy-start(f32[768]{0:T(1024)} %param.56) | copy-start | bytes 9220
  189.8 260.7 %all-reduce.11.cloned.1.call-start = ((), (), s32[]{:S(2)}) async-start(), calls=%async_computation.14 | async-start | bytes 6291456 | tf_op jit(solution)/shard_map/psum | solution.py:169
  314.0 282.4 %copy-start.56 = (f32[1024]{0:T(1024)}, f32[1024]{0:T(1024)S(1)}, u32[]{:S(2)}) copy-start(f32[1024]{0:T(1024)S(1)} %broadcast_multiply_fusion.1) | copy-start | bytes 12292
  316.2 134.3 %copy-start.63 = (f32[1024]{0:T(1024)}, f32[1024]{0:T(1024)S(1)}, u32[]{:S(2)}) copy-start(f32[1024]{0:T(1024)S(1)} %fusion.95) | copy-start | bytes 12292
  330.3 260.7 %all-reduce.13.cloned.1.call-start = ((), (), s32[]{:S(2)}) async-start(), calls=%async_computation.15 | async-start | bytes 6291456 | tf_op jit(solution)/shard_map/psum | solution.py:172
  470.7 279.5 %all-reduce.15.cloned.1.call-start = ((), (), s32[]{:S(2)}) async-start(), calls=%async_computation.16 | async-start | bytes 6291456 | tf_op jit(solution)/shard_map/psum | solution.py:172
  630.0 209.3 %reduce-scatter.51.cloned.1.call-start = ((), (), s32[]{:S(2)}) async-start(), calls=%async_computation.28 | async-start | bytes 884736
  634.0 234.1 %reduce-scatter.45.cloned.1.call-start = ((), (), s32[]{:S(2)}) async-start(), calls=%async_computation.25 | async-start | bytes 884736
  761.3 126.6 %reduce-scatter.29.cloned.1.call-start = ((), (), s32[]{:S(2)}) async-start(), calls=%async_computation.17 | async-start | bytes 3932160 | tf_op jit(solution)/shard_map/reduce_scatter | solution.py:175
  767.3 183.3 %reduce-scatter.37.cloned.1.call-start = ((), (), s32[]{:S(2)}) async-start(), calls=%async_computation.21 | async-start | bytes 3932160
  802.0 195.0 %reduce-scatter.35.cloned.1.call-start = ((), (), s32[]{:S(2)}) async-start(), calls=%async_computation.20 | async-start | bytes 2654208 | tf_op jit(solution)/shard_map/reduce_scatter | solution.py:309
  807.6 236.2 %reduce-scatter.33.cloned.1.call-start = ((), (), s32[]{:S(2)}) async-start(), calls=%async_computation.19 | async-start | bytes 2654208 | tf_op jit(solution)/shard_map/reduce_scatter | solution.py:308
  813.3 269.0 %reduce-scatter.31.cloned.1.call-start = ((), (), s32[]{:S(2)}) async-start(), calls=%async_computation.18 | async-start | bytes 884736 | tf_op jit(solution)/shard_map/reduce_scatter | solution.py:304
  815.9 305.2 %reduce-scatter.49.cloned.1.call-start = ((), (), s32[]{:S(2)}) async-start(), calls=%async_computation.27 | async-start | bytes 884736
  820.6 339.0 %reduce-scatter.47.cloned.1.call-start = ((), (), s32[]{:S(2)}) async-start(), calls=%async_computation.26 | async-start | bytes 884736
  825.3 373.0 %reduce-scatter.43.cloned.1.call-start = ((), (), s32[]{:S(2)}) async-start(), calls=%async_computation.24 | async-start | bytes 884736
  828.9 407.9 %reduce-scatter.39.cloned.1.call-start = ((), (), s32[]{:S(2)}) async-start(), calls=%async_computation.22 | async-start | bytes 884736
  833.5 441.9 %reduce-scatter.41.cloned.1.call-start = ((), (), s32[]{:S(2)}) async-start(), calls=%async_computation.23 | async-start | bytes 884736
  (116 other events, 1006.3 us)
Sparse Core Ops, SparseCore 0:
  40.4 123.7 all-reduce.6
  189.9 120.0 all-reduce.8
  330.4 120.0 all-reduce.10
  470.8 120.0 all-reduce.12
  630.0 120.0 all-reduce.14
  753.2 33.9 reduce-scatter.50
  790.3 34.9 reduce-scatter.44
  827.7 60.2 reduce-scatter.28
  890.3 60.2 reduce-scatter.36
  954.4 42.5 reduce-scatter.34
  1001.2 42.4 reduce-scatter.32
  1047.3 34.9 reduce-scatter.30
  1086.0 34.9 reduce-scatter.48
  1124.6 34.9 reduce-scatter.46
  1163.2 34.9 reduce-scatter.42
  1201.8 34.9 reduce-scatter.38
  1240.4 34.9 reduce-scatter.40
where the time goes:
time: 1290 us; the launch traced here: 1280 us
  waiting for transfers between devices  995 us (77%)
  matrix products  125 us (10%)
  other arithmetic  60.8 us (5%)
  local copies, waits for them, and re-layouts  52.4 us (4%)
  blocking collectives  25.8 us (2%)
  between operations  15.5 us (1%)
    psum x3, waiting for transfers between devices, branch_total(): return lax.psum(partial_term, 'tensor')  360 us
    unnamed x25, waiting for transfers between devices  254 us
    psum x2, waiting for transfers between devices, input_total(): return lax.psum(partial_term, 'tensor')  236 us
    reduce_scatter x1, waiting for transfers between devices, per_device(): lax.psum_scatter(ffn_summed[0], 'dp', scatter_dimension=0, tiled=True)  46.8 us
    reduce_scatter x1, waiting for transfers between devices, per_device(): lax.psum_scatter(ffn_summed[1], 'dp', scatter_dimension=1, tiled=True)  42.2 us
    reduce_scatter x1, waiting for transfers between devices, per_device(): lax.psum_scatter(cross_summed[0], 'dp', scatter_dimension=0, tiled=True)  38.6 us
    unnamed x199, local copies, waits for them, and re-layouts  31.8 us
    dot_general x10, matrix products, matmul(): return jnp.dot(left_side, right_side, preferred_element_type=jnp.float32)  30.7 us
  transfers between devices with their start and end apart: 17, of which 15 were waited for; matrix products, arithmetic and copies ran while one was open for 8% of the time, Pallas kernels for 0%

commit v1 on v0

--- a/solution.py
+++ b/solution.py
@@ -3,6 +3,7 @@
 import jax.numpy as jnp
 from jax import lax
 from jax.sharding import PartitionSpec as P
+from jax.lax import all_gather
 
 HEAD_DIM = 64
 EPSILON = 1e-05
@@ -169,7 +170,7 @@
         return lax.psum(partial_term, "tensor")
 
     def input_total(partial_term):
-        return lax.psum(partial_term, "tensor")
+        return all_gather(partial_term, "tensor").sum(axis=0)
 
     def edge_total(partial_term):
         return lax.psum_scatter(partial_term, "tensor", scatter_dimension=1, tiled=True)

time: 1290 us -> 1490 us (1.16)
  waiting for transfers between devices: 995 us -> 1180 us
    all_gather x0 -> x2, waiting for transfers between devices: none -> 425 us  [input_total(): return all_gather(partial_term, 'tensor').sum(axis=0)]
    psum x2 -> x0, waiting for transfers between devices: 236 us -> none  [input_total(): return lax.psum(partial_term, 'tensor')]
    reduce_sum x0 -> x2, other arithmetic: none -> 14.9 us  [input_total(): return all_gather(partial_term, 'tensor').sum(axis=0)]
    unnamed x199 -> x205, local copies, waits for them, and re-layouts: 31.8 us -> 33.1 us
  transfers between devices with their start and end apart: 17 -> 17, of which waited for: 15 -> 16; matrix products, arithmetic and copies ran while one was open for 8% -> 7% of each run, Pallas kernels for 0% -> 0%
where the time goes in v1:
time: 1490 us; the launch traced here: 1480 us
  waiting for transfers between devices  1180 us (79%)
  matrix products  127 us (9%)
  other arithmetic  73.4 us (5%)
  local copies, waits for them, and re-layouts  54.4 us (4%)
  blocking collectives  25 us (2%)
  between operations  15.3 us (1%)
    all_gather x2, waiting for transfers between devices, input_total(): return all_gather(partial_term, 'tensor').sum(axis=0)  425 us
    psum x3, waiting for transfers between devices, branch_total(): return lax.psum(partial_term, 'tensor')  360 us
    unnamed x25, waiting for transfers between devices  265 us
    reduce_scatter x1, waiting for transfers between devices, per_device(): lax.psum_scatter(ffn_summed[0], 'dp', scatter_dimension=0, tiled=True)  46.8 us
    reduce_scatter x1, waiting for transfers between devices, per_device(): lax.psum_scatter(ffn_summed[1], 'dp', scatter_dimension=1, tiled=True)  42.1 us
    reduce_scatter x1, waiting for transfers between devices, per_device(): lax.psum_scatter(cross_summed[0], 'dp', scatter_dimension=0, tiled=True)  38.6 us
    unnamed x205, local copies, waits for them, and re-layouts  33.1 us
    dot_general x10, matrix products, matmul(): return jnp.dot(left_side, right_side, preferred_element_type=jnp.float32)  30.7 us
  transfers between devices with their start and end apart: 17, of which 16 were waited for; matrix products, arithmetic and copies ran while one was open for 7% of the time, Pallas kernels for 0%

profile of v1, /device:TPU:0, one launch (start us, length us, event | category | flops | bytes accessed | tf_op | source)
XLA Modules:
  0.0 1484.1 jit_solution(11295316932334717814)
XLA Ops:
  15.3 19.3 %while.96 = (s32[]{:T(128)}, bf16[2,512,3,64]{1,3,2,0:T(8,128)(2,1)}, f32[2,3,512]{2,1,0:T(4,128)}, s32[2]{0:T(128)S(1)}, s32[1024]{0:T(1024)S(1)}, /*index=5*/b...) while((s32[]{:T(128)}, ...), condition=%wide.region_3.4_spmd, body=%wide.region_0.3_spmd.sunk | while | flops 423197696 | bytes 27042136 | solution.py:76
  44.9 119.4 %all-reduce.5.cloned.1.call-done = f32[1024,768]{1,0:T(8,128)} async-done(((f32[1024,768]{1,0:T(8,128)}), f32[1024,768]{1,0:T(8,128)}) %all-reduce.5.cloned.1.call-update) | async-done | bytes 3145744 | tf_op jit(solution)/shard_map/psum | solution.py:170
  170.4 14.2 while.97
  190.0 120.0 %all-reduce.7.cloned.1.call-done = f32[1024,768]{1,0:T(8,128)} async-done(((f32[1024,768]{1,0:T(8,128)}), f32[1024,768]{1,0:T(8,128)}) %all-reduce.7.cloned.1.call-update) | async-done | bytes 3145744 | tf_op jit(solution)/shard_map/psum | solution.py:170
  316.1 9.8 multiply_convert_fusion.2
  330.3 120.2 %all-reduce.9.cloned.1.call-done = f32[1024,768]{1,0:T(8,128)} async-done(((f32[1024,768]{1,0:T(8,128)}), f32[1024,768]{1,0:T(8,128)}) %all-reduce.9.cloned.1.call-update) | async-done | bytes 3145744 | tf_op jit(solution)/shard_map/psum | solution.py:170
  471.1 216.9 %all-gather.5.cloned.1.call-done = f32[4096,768]{1,0:T(8,128)} async-done(((f32[1024,768]{1,0:T(8,128)}), f32[4096,768]{1,0:T(8,128)}) %all-gather.5.cloned.1.call-update) | async-done | bytes 12582928 | tf_op jit(solution)/shard_map/all_gather | solution.py:173
  688.0 7.5 reduce_sum.354
  706.4 25.0 %while.98 = (s32[]{:T(128)}, f32[1024,3,64]{0,2,1:T(8,128)S(1)}, f32[1024,3,64]{0,2,1:T(8,128)}, bf16[2,512,3,64]{1,3,2,0:T(8,128)(2,1)}, s32[2]{0:T(128)}, /*in...) while((s32[]{:T(128)}, f32[1024,3,64]{0,2,1:T(8,128)S(1)}, ...), condition=%wide.region_24.25_spmd.clone, body=%wide.region_22.24_spmd.clone.sunk | while | flops 1031928320 | bytes 65659268 | solution.py:116
  745.0 207.9 %all-gather.7.cloned.1.call-done = f32[4096,768]{1,0:T(8,128)} async-done(((f32[1024,768]{1,0:T(8,128)}), f32[4096,768]{1,0:T(8,128)}) %all-gather.7.cloned.1.call-update) | async-done | bytes 12582928 | tf_op jit(solution)/shard_map/all_gather | solution.py:173
  952.9 7.4 reduce_sum.357
  972.3 24.2 %while.99 = (s32[]{:T(128)}, f32[1024,3,64]{0,2,1:T(8,128)S(1)}, f32[1024,3,64]{0,2,1:T(8,128)}, bf16[2,512,3,64]{1,3,2,0:T(8,128)(2,1)}, s32[2]{0:T(128)S(1)}, ...) while((s32[]{:T(128)}, f32[1024,3,64]{0,2,1:T(8,128)S(1)}, ...), condition=%wide.region_30.31_spmd.clone, body=%wide.region_28.30_spmd.clone.sunk | while | flops 1032977408 | bytes 65663364 | solution.py:116
  1014.2 5.6 fusion.106
  1054.1 25.0 %all-reduce = (f32[192]{0:T(256)}, f32[192]{0:T(256)}, f32[768]{0:T(1024)}, f32[768]{0:T(1024)}, f32[768]{0:T(1024)}, /*index=5*/f32[192]{0:T(256)}, f32[192]{0:...) all-reduce(f32[192]{0:T(256)S(1)} %reduce_sum.361, ...), channel_id=1, replica_groups=mesh['dp'=8,'tensor'=4] {'dp'}, use_global_device_ids=true, to_apply=%region_35.36 | all-reduce | flops 8448 | bytes 67584 | tf_op jit(solution)/shard_map/psum | solution.py:312
  1079.0 10.9 reduce-scatter.45.cloned.1.call-done
  1091.6 61.0 %reduce-scatter.37.cloned.1.call-done = f32[192,1024]{1,0:T(8,128)} async-done(((f32[768,1024]{1,0:T(8,128)}), f32[192,1024]{1,0:T(8,128)}) %reduce-scatter.37.cloned.1.call-update) | async-done | bytes 786448
  1156.7 42.1 %reduce-scatter.35.cloned.1.call-done = f32[768,96]{0,1:T(8,128)} async-done(((f32[768,768]{0,1:T(8,128)}), f32[768,96]{0,1:T(8,128)}) %reduce-scatter.35.cloned.1.call-update) | async-done | bytes 294928 | tf_op jit(solution)/shard_map/reduce_scatter | solution.py:310
  1198.8 46.8 %reduce-scatter.33.cloned.1.call-done = f32[96,768]{1,0:T(8,128)} async-done(((f32[768,768]{1,0:T(8,128)}), f32[96,768]{1,0:T(8,128)}) %reduce-scatter.33.cloned.1.call-update) | async-done | bytes 294928 | tf_op jit(solution)/shard_map/reduce_scatter | solution.py:309
  1245.6 38.6 %reduce-scatter.31.cloned.1.call-done = f32[96,192]{1,0:T(8,128)} async-done(((f32[768,192]{1,0:T(8,128)}), f32[96,192]{1,0:T(8,128)}) %reduce-scatter.31.cloned.1.call-update) | async-done | bytes 73744 | tf_op jit(solution)/shard_map/reduce_scatter | solution.py:305
  1284.2 38.7 %reduce-scatter.49.cloned.1.call-done = f32[96,192]{1,0:T(8,128)} async-done(((f32[768,192]{1,0:T(8,128)}), f32[96,192]{1,0:T(8,128)}) %reduce-scatter.49.cloned.1.call-update) | async-done | bytes 73744
  1323.0 38.6 %reduce-scatter.47.cloned.1.call-done = f32[96,192]{1,0:T(8,128)} async-done(((f32[768,192]{1,0:T(8,128)}), f32[96,192]{1,0:T(8,128)}) %reduce-scatter.47.cloned.1.call-update) | async-done | bytes 73744
  1361.6 38.6 %reduce-scatter.43.cloned.1.call-done = f32[96,192]{1,0:T(8,128)} async-done(((f32[768,192]{1,0:T(8,128)}), f32[96,192]{1,0:T(8,128)}) %reduce-scatter.43.cloned.1.call-update) | async-done | bytes 73744
  1400.2 38.6 %reduce-scatter.39.cloned.1.call-done = f32[96,192]{1,0:T(8,128)} async-done(((f32[768,192]{1,0:T(8,128)}), f32[96,192]{1,0:T(8,128)}) %reduce-scatter.39.cloned.1.call-update) | async-done | bytes 73744
  1438.8 38.6 %reduce-scatter.41.cloned.1.call-done = f32[96,192]{1,0:T(8,128)} async-done(((f32[768,192]{1,0:T(8,128)}), f32[96,192]{1,0:T(8,128)}) %reduce-scatter.41.cloned.1.call-update) | async-done | bytes 73744
  (459 shorter events, 230.6 us)
Async XLA Ops:
  7.2 157.0 %all-reduce.5.cloned.1.call-start = ((), (), s32[]{:S(2)}) async-start(), calls=%async_computation.12 | async-start | bytes 6291456 | tf_op jit(solution)/shard_map/psum | solution.py:170
  40.3 123.9 %copy-start.92 = (f32[768]{0:T(1024)S(1)}, f32[768]{0:T(1024)}, u32[]{:S(2)}) copy-start(f32[768]{0:T(1024)} %param.47) | copy-start | bytes 9220
  40.3 269.7 %all-reduce.7.cloned.1.call-start = ((), (), s32[]{:S(2)}) async-start(), calls=%async_computation.13 | async-start | bytes 6291456 | tf_op jit(solution)/shard_map/psum | solution.py:170
  168.1 141.9 %copy-start.63 = (f32[1024]{0:T(1024)}, f32[1024]{0:T(1024)S(1)}, u32[]{:S(2)}) copy-start(f32[1024]{0:T(1024)S(1)} %fusion.94) | copy-start | bytes 12292
  186.4 123.6 %copy-start.66 = (f32[768]{0:T(1024)S(1)}, f32[768]{0:T(1024)}, u32[]{:S(2)}) copy-start(f32[768]{0:T(1024)} %param.48) | copy-start | bytes 9220
  186.4 123.6 %copy-start.84 = (f32[768]{0:T(1024)S(1)}, f32[768]{0:T(1024)}, u32[]{:S(2)}) copy-start(f32[768]{0:T(1024)} %param.49) | copy-start | bytes 9220
  186.4 123.6 %copy-start.93 = (f32[768]{0:T(1024)S(1)}, f32[768]{0:T(1024)}, u32[]{:S(2)}) copy-start(f32[768]{0:T(1024)} %param.56) | copy-start | bytes 9220
  189.8 260.7 %all-reduce.9.cloned.1.call-start = ((), (), s32[]{:S(2)}) async-start(), calls=%async_computation.14 | async-start | bytes 6291456 | tf_op jit(solution)/shard_map/psum | solution.py:170
  313.9 387.0 %copy-start.61 = (f32[1024]{0:T(1024)}, f32[1024]{0:T(1024)S(1)}, u32[]{:S(2)}) copy-start(f32[1024]{0:T(1024)S(1)} %broadcast_multiply_fusion.1) | copy-start | bytes 12292
  316.1 134.3 %copy-start.68 = (f32[1024]{0:T(1024)}, f32[1024]{0:T(1024)S(1)}, u32[]{:S(2)}) copy-start(f32[1024]{0:T(1024)S(1)} %fusion.95) | copy-start | bytes 12292
  330.2 357.8 %all-gather.5.cloned.1.call-start = ((), (), s32[]{:S(2)}) async-start(), calls=%async_computation.19 | async-start | bytes 15728640 | tf_op jit(solution)/shard_map/all_gather | solution.py:173
  470.6 482.3 %all-gather.7.cloned.1.call-start = ((), (), s32[]{:S(2)}) async-start(), calls=%async_computation.20 | async-start | bytes 15728640 | tf_op jit(solution)/shard_map/all_gather | solution.py:173
  736.4 309.5 %reduce-scatter.51.cloned.1.call-start = ((), (), s32[]{:S(2)}) async-start(), calls=%async_computation.28 | async-start | bytes 884736
  739.8 311.9 %reduce-scatter.29.cloned.1.call-start = ((), (), s32[]{:S(2)}) async-start(), calls=%async_computation.15 | async-start | bytes 3932160 | tf_op jit(solution)/shard_map/reduce_scatter | solution.py:176
  745.0 345.0 %reduce-scatter.45.cloned.1.call-start = ((), (), s32[]{:S(2)}) async-start(), calls=%async_computation.25 | async-start | bytes 884736
  1003.1 149.4 %reduce-scatter.37.cloned.1.call-start = ((), (), s32[]{:S(2)}) async-start(), calls=%async_computation.21 | async-start | bytes 3932160
  1008.4 190.4 %reduce-scatter.35.cloned.1.call-start = ((), (), s32[]{:S(2)}) async-start(), calls=%async_computation.18 | async-start | bytes 2654208 | tf_op jit(solution)/shard_map/reduce_scatter | solution.py:310
  1014.1 231.5 %reduce-scatter.33.cloned.1.call-start = ((), (), s32[]{:S(2)}) async-start(), calls=%async_computation.17 | async-start | bytes 2654208 | tf_op jit(solution)/shard_map/reduce_scatter | solution.py:309
  1019.9 264.3 %reduce-scatter.31.cloned.1.call-start = ((), (), s32[]{:S(2)}) async-start(), calls=%async_computation.16 | async-start | bytes 884736 | tf_op jit(solution)/shard_map/reduce_scatter | solution.py:305
  1022.5 300.5 %reduce-scatter.49.cloned.1.call-start = ((), (), s32[]{:S(2)}) async-start(), calls=%async_computation.27 | async-start | bytes 884736
  1027.2 334.3 %reduce-scatter.47.cloned.1.call-start = ((), (), s32[]{:S(2)}) async-start(), calls=%async_computation.26 | async-start | bytes 884736
  1031.9 368.3 %reduce-scatter.43.cloned.1.call-start = ((), (), s32[]{:S(2)}) async-start(), calls=%async_computation.24 | async-start | bytes 884736
  1035.5 403.3 %reduce-scatter.39.cloned.1.call-start = ((), (), s32[]{:S(2)}) async-start(), calls=%async_computation.22 | async-start | bytes 884736
  1040.2 437.2 %reduce-scatter.41.cloned.1.call-start = ((), (), s32[]{:S(2)}) async-start(), calls=%async_computation.23 | async-start | bytes 884736
  (119 other events, 625.6 us)
Sparse Core Ops, SparseCore 0:
  40.4 123.7 all-reduce.4
  189.9 120.0 all-reduce.6
  330.3 120.0 all-reduce.8
  470.8 217.2 all-gather.4
  736.5 216.3 all-gather.6
  955.9 33.2 reduce-scatter.50
  991.5 60.2 reduce-scatter.28
  1054.9 35.0 reduce-scatter.44
  1092.3 60.2 reduce-scatter.36
  1156.3 42.4 reduce-scatter.34
  1203.1 42.4 reduce-scatter.32
  1249.2 34.9 reduce-scatter.30
  1288.0 34.9 reduce-scatter.48
  1326.6 34.9 reduce-scatter.46
  1365.2 34.9 reduce-scatter.42
  1403.8 34.9 reduce-scatter.38
  1442.4 34.9 reduce-scatter.40
